TPU v7x, 128 devices: a whole 4x4x4 slice. The times are simulated.
128 devices in a mesh: rows: 8 (over z_hi, y), cols: 16 (over z_lo, x, core).
Axes of the slice: x: 4, y: 4, z: 4 (z_hi: 2, z_lo: 2; z = z_hi * 2 + z_lo), core: 2. Of those that a mesh axis runs over, the one named last changes fastest.
Arguments:
- dosage: int32 [512, 24576], P('cols', 'rows'), may hold values from 0 to 2
- present: int32 [512, 24576], P('cols', 'rows'), may hold values from 0 to 1, as said below
- components: float32 [32, 24576], P(None, 'rows'), may hold values from -8 to 8
Outputs:
- kinship: float32 [24576, 24576], P('rows', 'cols')
Inputs may be any that keep to these rules, and one draw needn't show every extreme that they name: `present`: markers whose index is a multiple of 8 are observed for every person.
All inputs are finite; a program needn't handle non-finite values.
Results may differ from a plain program's by a relative error of at most 0.0036.
Values may be sent and summed in bfloat16 or wider, within the bound.
A program may use at most 128 MiB of HBM per device.

v0:
```python
import jax
import jax.numpy as jnp
from jax import lax
from jax.sharding import PartitionSpec as P


def broadcast(block, axis, holder):
    block = jnp.where(lax.axis_index(axis) == holder, block, jnp.zeros_like(block))
    return lax.psum(block, axis)


def solve_normal(gram, moment):
    width = gram.shape[0]
    index_col = jnp.arange(width, dtype=jnp.int32)[:, None]
    columns = []
    for j in range(width):
        column = gram[:, j, :]
        if j > 0:
            stacked = jnp.stack(columns, axis=1)
            column = column - jnp.sum(stacked * stacked[j][None, :, :], axis=1)
        pivot = jnp.sqrt(column[j])
        columns.append(jnp.where(index_col >= j, column / pivot[None, :], jnp.zeros_like(column)))
    factor = jnp.stack(columns, axis=1)
    forward = []
    for j in range(width):
        value = moment[j]
        for k in range(j):
            value = value - factor[j, k] * forward[k]
        forward.append(value / factor[j, j])
    backward = [None] * width
    for j in range(width - 1, -1, -1):
        value = forward[j]
        for k in range(j + 1, width):
            value = value - factor[k, j] * backward[k]
        backward[j] = value / factor[j, j]
    return jnp.stack(backward, axis=0)


def per_device(dosage, present, components):
    people = components.shape[1]
    design = jnp.concatenate([jnp.ones((1, people), jnp.float32), components], axis=0)
    width = design.shape[0]
    observed = present.astype(jnp.float32)
    counts = dosage.astype(jnp.float32)
    target = 0.5 * counts * observed
    outer_rows = (design[:, None, :] * design[None, :, :]).reshape(width * width, people)
    gram_part = jnp.dot(
        outer_rows, observed.T, precision=lax.Precision.HIGHEST, preferred_element_type=jnp.float32
    )
    moment_part = jnp.dot(
        design, target.T, precision=lax.Precision.HIGHEST, preferred_element_type=jnp.float32
    )
    gram_flat, moment = lax.psum((gram_part, moment_part), "rows")
    markers_here = observed.shape[0]
    gram = gram_flat.reshape(width, width, markers_here)
    coef = solve_normal(gram, moment)
    fitted = jnp.dot(
        coef.T, design, precision=lax.Precision.HIGHEST, preferred_element_type=jnp.float32
    )
    freq = jnp.clip(fitted, 0.01, 0.99)
    resid = observed * (counts - 2.0 * freq)
    sdev = observed * jnp.sqrt(freq * (1.0 - freq))
    panel = jnp.stack([resid, sdev]).astype(jnp.bfloat16)
    ratio = lax.axis_size("cols") // lax.axis_size("rows")
    column_width = people // ratio
    col_index = lax.axis_index("cols")
    col_start = col_index % ratio * column_width
    owner = col_index // ratio
    contract = (((0,), (0,)), ((), ()))
    full_rows = lax.all_gather(panel, "cols", axis=1, tiled=True)
    own_part = lax.dynamic_slice_in_dim(full_rows, col_start, column_width, 2)
    full_cols = broadcast(own_part, "rows", owner)
    numer = lax.dot_general(
        full_rows[0], full_cols[0], contract, preferred_element_type=jnp.float32
    )
    denom = lax.dot_general(
        full_rows[1], full_cols[1], contract, preferred_element_type=jnp.float32
    )
    return numer / (4.0 * denom)


def solution(mesh):
    placed = (P("cols", "rows"), P("cols", "rows"), P(None, "rows"))
    return jax.shard_map(
        per_device, mesh=mesh, in_specs=placed, out_specs=P("rows", "cols"), check_vma=False
    )
```

profile of v0, /device:TPU:1, one launch (start us, length us, event | category | flops | bytes accessed | tf_op | source)
XLA Modules:
  0.0 335.1 jit_solution(12750329239006864521)
XLA Ops:
  6.5 1.0 concatenate.3
  7.6 8.0 %broadcast_multiply_fusion = f32[33,33,3072]{2,1,0:T(8,128)} fusion(f32[33,3072]{1,0:T(8,128)S(1)} %concatenate.3), kind=kLoop, calls=%fused_computation.1 | loop fusion | flops 3345408 | bytes 13787136 | tf_op jit(solution)/shard_map/mul | solution.py:46
  15.6 10.5 %mul.11354 = f32[1089,3072]{1,0:T(8,128)} reshape(f32[33,33,3072]{2,1,0:T(8,128)} %broadcast_multiply_fusion) | data formatting | bytes 26763264 | tf_op jit(solution)/shard_map/mul | solution.py:46
  26.1 14.2 %fusion.8 = f32[1089,32]{0,1:T(8,128)S(1)} fusion(f32[1089,3072]{1,0:T(8,128)} %mul.11354, s32[32,3072]{1,0:T(8,128)S(1)} %copy-done.1), kind=kOutput, calls=%fused_computation.550 | convolution fusion | flops 1284734976 | bytes 13914240 | tf_op jit(solution)/shard_map/dot_general | solution.py:47
  40.3 0.2 reshape.1737
  40.6 1.2 copy.48
  42.2 0.6 fusion.4
  42.8 0.6 slice.4598
  43.4 37.2 %psum.21 = f32[33,32]{1,0:T(8,128)S(1)} all-reduce(f32[33,32]{1,0:T(8,128)S(1)} %fusion.4), channel_id=1, replica_groups=mesh['rows'=8,'cols'=16] {'rows'}, use_global_device_ids=true, to_apply=%region_0.0 | all-reduce | flops 1056 | bytes 8448 | tf_op jit(solution)/shard_map/psum | solution.py:53
  80.6 45.4 %all-reduce.4.cloned.1.call-done = f32[33,33,32]{2,0,1:T(8,128)} async-done(((f32[33,33,32]{2,0,1:T(8,128)}), f32[33,33,32]{2,0,1:T(8,128)}) %all-reduce.4.cloned.1.call-update) | async-done | bytes 139408 | tf_op jit(solution)/shard_map/psum | solution.py:53
  126.0 0.8 fusion.113
  126.8 0.7 bitcast_divide_fusion.1
  127.5 0.7 constant_dynamic-update-slice_fusion.517
  128.3 0.8 constant_dynamic-update-slice_fusion.454
  129.2 0.7 bitcast_subtract_fusion.59
  130.0 0.8 constant_dynamic-update-slice_fusion.79
  130.9 0.7 bitcast_subtract_fusion.58
  131.7 0.8 constant_dynamic-update-slice_fusion.514
  132.6 0.7 bitcast_subtract_fusion.56
  133.4 0.8 constant_dynamic-update-slice_fusion.513
  134.3 0.7 bitcast_subtract_fusion.54
  135.1 0.8 constant_dynamic-update-slice_fusion.512
  136.0 0.7 bitcast_subtract_fusion.52
  136.8 0.8 constant_dynamic-update-slice_fusion.511
  137.7 0.7 bitcast_subtract_fusion.50
  138.5 0.8 constant_dynamic-update-slice_fusion.510
  139.4 0.7 bitcast_subtract_fusion.48
  140.2 0.8 constant_dynamic-update-slice_fusion.509
  141.1 0.7 bitcast_subtract_fusion.46
  141.9 0.8 constant_dynamic-update-slice_fusion.508
  142.8 0.7 bitcast_subtract_fusion.44
  143.6 0.8 constant_dynamic-update-slice_fusion.507
  150.9 0.1 multiply_reduce_fusion.1
  151.0 0.4 subtract_divide_fusion.12
  151.4 0.4 bitcast_divide_fusion.3
  151.9 0.1 multiply_reduce_fusion
  152.0 0.8 fusion.144
  152.8 0.6 fusion.1200
  153.4 0.8 subtract_divide_fusion
  154.2 0.1 stack.167
  154.3 0.7 fusion.11
  155.0 0.8 pad_maximum_fusion
  155.9 0.3 all-reduce.6.cloned.1.call-start
  156.1 46.4 %all-gather.2.cloned.1.call-done = bf16[2,512,3072]{2,1,0:T(8,128)(2,1)} async-done(((bf16[2,32,3072]{2,1,0:T(8,128)(2,1)}), bf16[2,512,3072]{2,1,0:T(8,128)(2,1)}) %all-gather.2.cloned.1.call-update) | async-done | bytes 6291472 | tf_op jit(solution)/shard_map/all_gather | solution.py:70
  202.5 4.1 %dynamic-slice_select_fusion = bf16[2,512,1536]{2,1,0:T(8,128)(2,1)} fusion(bf16[2,512,3072]{2,1,0:T(8,128)(2,1)} %all-gather.2.cloned.1.call-done, s32[]{:T(128)S(6)} %select_n.281, pred[]{:T(512)S(6)} %eq.5), kind=kLoop, calls=%fused_computation.6 | loop fusion | flops 1572864 | bytes 6291461 | tf_op jit(solution)/shard_map/jit(_where)/select_n | solution.py:8
  206.6 96.2 %all-reduce.6.cloned.1.call-done = bf16[2,512,1536]{2,1,0:T(8,128)(2,1)} async-done(((bf16[2,512,1536]{2,1,0:T(8,128)(2,1)}), bf16[2,512,1536]{2,1,0:T(8,128)(2,1)}) %all-reduce.6.cloned.1.call-update) | async-done | bytes 3145744 | tf_op jit(solution)/shard_map/psum | solution.py:9
  302.8 11.7 %fusion = f32[3072,1536]{1,0:T(8,128)} fusion(bf16[2,512,3072]{2,1,0:T(8,128)(2,1)} %all-gather.2.cloned.1.call-done, bf16[2,512,1536]{2,1,0:T(8,128)(2,1)} %all-reduce.6.cloned.1.call-done), kind=kOutput, calls=%fused_computation.5 | convolution fusion | flops 4831838208 | bytes 23592960 | tf_op jit(solution)/shard_map/dot_general | solution.py:73
  314.5 14.1 %multiply_divide_fusion = f32[3072,1536]{1,0:T(8,128)} fusion(f32[3072,1536]{1,0:T(8,128)} %fusion, bf16[2,512,3072]{2,1,0:T(8,128)(2,1)} %all-gather.2.cloned.1.call-done, bf16[2,512,1536]{2,1,0:T(8,128)(2,1)S(1)} %copy-done.4), kind=kOutput, calls=%fused_computation | convolution fusion | flops 4841275392 | bytes 42467328 | tf_op jit(solution)/shard_map/dot_general | solution.py:76
  (281 shorter events, 7.3 us)
Async XLA Ops:
  6.5 119.5 %all-reduce.4.cloned.1.call-start = ((), (), s32[]{:S(2)}) async-start(), calls=%async_computation | async-start | bytes 1351680 | tf_op jit(solution)/shard_map/psum | solution.py:53
  15.6 10.6 %copy-start.1 = (s32[32,3072]{1,0:T(8,128)S(1)}, s32[32,3072]{1,0:T(8,128)}, u32[]{:S(2)}) copy-start(s32[32,3072]{1,0:T(8,128)} %param.4) | copy-start | bytes 1179652
  26.1 16.1 %copy-start = (f32[32,3072]{1,0:T(8,128)S(1)}, f32[32,3072]{1,0:T(8,128)}, u32[]{:S(2)}) copy-start(f32[32,3072]{1,0:T(8,128)} %param.5) | copy-start | bytes 1179652
  26.1 16.1 %copy-start.3 = (s32[32,3072]{1,0:T(8,128)S(1)}, s32[32,3072]{1,0:T(8,128)}, u32[]{:S(2)}) copy-start(s32[32,3072]{1,0:T(8,128)} %param.3) | copy-start | bytes 1179652
  41.8 160.7 %all-gather.2.cloned.1.call-start = ((), (), s32[]{:S(2)}) async-start(), calls=%async_computation.1 | async-start | bytes 6684672 | tf_op jit(solution)/shard_map/all_gather | solution.py:70
  126.0 18.4 %copy-start.2 = (f32[33,33,32]{2,0,1:T(8,128)S(1)}, f32[33,33,32]{2,0,1:T(8,128)}, u32[]{:S(2)}) copy-start(f32[33,33,32]{2,0,1:T(8,128)} %all-reduce.4.cloned.1.call-done) | copy-start | bytes 418180
  155.9 147.0 %all-reduce.6.cloned.1.call-start = ((), (), s32[]{:S(2)}) async-start(), calls=%async_computation.2 | async-start | bytes 6291456 | tf_op jit(solution)/shard_map/psum | solution.py:9
  302.8 11.7 %copy-start.4 = (bf16[2,512,1536]{2,1,0:T(8,128)(2,1)S(1)}, bf16[2,512,1536]{2,1,0:T(8,128)(2,1)}, u32[]{:S(2)}) copy-start(bf16[2,512,1536]{2,1,0:T(8,128)(2,1)} %all-reduce.6.cloned.1.call-done) | copy-start | bytes 9437188
Sparse Core Ops, SparseCore 0:
  41.9 84.0 all-reduce.3
  156.0 46.4 all-gather.1
  206.7 96.0 all-reduce.5
where the time goes:
time: 340 us; the launch traced here: 335 us
  waiting for transfers between devices  188 us (55%)
  matrix products  41.3 us (12%)
  other arithmetic  37.7 us (11%)
  blocking collectives  37.2 us (11%)
  local copies, waits for them, and re-layouts  16.1 us (5%)
  between operations  14.6 us (4%)
    psum x1, waiting for transfers between devices, broadcast(): return lax.psum(block, axis)  96.2 us
    all_gather x1, waiting for transfers between devices, per_device(): full_rows = lax.all_gather(panel, 'cols', axis=1, tiled=True)  46.4 us
    psum x1, waiting for transfers between devices, per_device(): gram_flat, moment = lax.psum((gram_part, moment_part), 'rows')  45.4 us
    psum x1, blocking collectives, per_device(): gram_flat, moment = lax.psum((gram_part, moment_part), 'rows')  37.2 us
    dot_general x1, matrix products, per_device(): jnp.dot(outer_rows, observed.T, precision=lax.Precision.HIGHEST, preferre...  14.2 us
    dot_general x1, matrix products, per_device(): lax.dot_general(full_rows[1], full_cols[1], contract, preferred_element_t...  14.1 us
    dot_general x1, matrix products, per_device(): lax.dot_general(full_rows[0], full_cols[0], contract, preferred_element_t...  11.7 us
    mul x1, local copies, waits for them, and re-layouts, per_device(): design[:, None, :] * design[None, :, :]  10.5 us
  transfers between devices with their start and end apart: 3, of which 3 were waited for; matrix products, arithmetic and copies ran while one was open for 0% of the time, Pallas kernels for 0%

commit v1 on v0

v1 whole, which is shorter than its diff:
```python
import functools

import jax
import jax.numpy as jnp
from jax import lax
from jax.experimental import pallas as pl
from jax.experimental.pallas import tpu as pltpu
from jax.sharding import PartitionSpec as P

F32 = jnp.float32
BF16 = jnp.bfloat16
MESH = pl.DeviceIdType.MESH

COMPS = 32
WIDTH = 40
CHUNK = 512
OFF = []
for _i in range(COMPS + 1):
    OFF.append(sum(8 * (k // 8 + 1) for k in range(_i)))
GRAM_ROWS = 768
SUMS = 896


def rows_of(i):
    return 8 * (i // 8 + 1)


def split3(value):
    hi = value.astype(BF16).astype(F32)
    rest = value - hi
    mid = rest.astype(BF16).astype(F32)
    low = (rest - mid).astype(BF16).astype(F32)
    return hi, mid, low


def gram_sums(design, own, outer, acc):
    people = design.shape[1]
    acc[...] = jnp.zeros_like(acc)
    outer[OFF[COMPS] + WIDTH:, :] = jnp.zeros((GRAM_ROWS - OFF[COMPS] - WIDTH, CHUNK), F32)

    def chunk(step, carry):
        at = pl.ds(pl.multiple_of(step * CHUNK, CHUNK), CHUNK)
        for i in range(COMPS + 1):
            n = rows_of(i)
            outer[OFF[i]:OFF[i] + n, :] = design[0:n, at] * design[i:i + 1, at]
        left = own[:, :, at].reshape(64, CHUNK)
        value = outer[...]
        total = acc[...]
        for _ in range(3):
            piece = value.astype(BF16)
            total += lax.dot_general(
                left, piece, (((1,), (1,)), ((), ())), preferred_element_type=F32
            )
            value = value - piece.astype(F32)
        acc[...] = total
        return carry

    lax.fori_loop(0, people // CHUNK, chunk, 0)


def solve(gt, bt, inv_s, y_s, xs):
    for j in range(COMPS, -1, -1):
        n = rows_of(j)
        base = OFF[j]
        pivot = gt[pl.ds(base + j, 8, stride=0), :]
        inv = lax.rsqrt(pivot)
        inv = inv * (1.5 - 0.5 * pivot * inv * inv)
        inv_s[j] = inv
        column = [gt[base + 8 * q:base + 8 * q + 8, :] * inv for q in range(n // 8)]
        for q in range(n // 8):
            gt[base + 8 * q:base + 8 * q + 8, :] = column[q]
        y = bt[pl.ds(j, 8, stride=0), :] * inv
        y_s[j] = y
        for q in range(n // 8):
            bt[8 * q:8 * q + 8, :] = bt[8 * q:8 * q + 8, :] - y * column[q]
        for i in range(j - 1, -1, -1):
            factor = gt[pl.ds(base + i, 8, stride=0), :]
            for q in range(i // 8 + 1):
                lo = OFF[i] + 8 * q
                gt[lo:lo + 8, :] = gt[lo:lo + 8, :] - factor * column[q]
    sub = lax.broadcasted_iota(jnp.int32, (8, 128), 0)
    x = [jnp.zeros((8, 128), F32) for _ in range(WIDTH // 8)]
    for j in range(COMPS + 1):
        value = y_s[j]
        if j > 0:
            total = gt[OFF[j]:OFF[j] + 8, :] * x[0]
            for q in range(1, rows_of(j) // 8):
                total += gt[OFF[j] + 8 * q:OFF[j] + 8 * q + 8, :] * x[q]
            value = value - jnp.sum(total, axis=0, keepdims=True)
        value = value * inv_s[j]
        x[j // 8] = jnp.where(sub == j % 8, value, x[j // 8])
    twice = jnp.concatenate(x, axis=0) * 2.0
    hi, mid, low = split3(twice)
    for t, part in enumerate((hi, hi, hi, mid, mid, low)):
        xs[WIDTH * t:WIDTH * t + WIDTH, :] = part
    xs[6 * WIDTH:, :] = jnp.zeros((256 - 6 * WIDTH, 128), F32)


def gather_kernel(dosage, present, comps, a_out, b_out, cb_out, coef_out,
                  own, design, outer, acc, send, recv, wide, gt, bt, inv_s, y_s, xs, coef,
                  ssem, rsem, lsem):
    r = lax.axis_index("rows")
    c = lax.axis_index("cols")
    zh, y = r // 4, r % 4
    zl, x, k = c // 8, (c // 2) % 4, c % 2
    people = dosage.shape[1]
    half = people // 2

    def col(zl_, x_, k_):
        return zl_ * 8 + x_ * 2 + k_

    def row(zh_, y_):
        return zh_ * 4 + y_

    xr, xl, xo = (x + 1) % 4, (x + 3) % 4, (x + 2) % 4
    yr, yl, yo = (y + 1) % 4, (y + 3) % 4, (y + 2) % 4
    zlo, zho, ko = 1 - zl, 1 - zh, 1 - k
    t_row, t_chip = row(zl, x), col(zh, y, 0)
    away = jnp.logical_or(x != y, zh != zl)

    barrier = pltpu.get_barrier_semaphore()
    for d in range(1, 8):
        pl.semaphore_signal(barrier, inc=1, device_id=((r + d) % 8, c), device_id_type=MESH)
    for d in range(1, 16):
        pl.semaphore_signal(barrier, inc=1, device_id=(r, (c + d) % 16), device_id_type=MESH)

    @pl.when(away)
    def _():
        for q in range(2):
            pl.semaphore_signal(barrier, inc=1, device_id=(t_row, t_chip + q), device_id_type=MESH)

    seen = present[...].astype(F32)
    own[0] = (dosage[...].astype(F32) * seen).astype(BF16)
    own[1] = seen.astype(BF16)
    design[0:COMPS, :] = comps[...]
    sub = lax.broadcasted_iota(jnp.int32, (8, people), 0)
    design[COMPS:WIDTH, :] = jnp.where(sub == 0, 1.0, 0.0).astype(F32)

    pl.semaphore_wait(barrier, jnp.where(away, 24, 22))

    sent = []

    def copy(src, dst, idx, dev):
        return pltpu.make_async_remote_copy(
            src_ref=src, dst_ref=dst, send_sem=ssem.at[idx], recv_sem=rsem.at[idx],
            device_id=dev, device_id_type=MESH,
        )

    def push(src, dst, idx, dev):
        one = copy(src, dst, idx, dev)
        one.start()
        sent.append(one)

    def arrive(ref, idx):
        copy(ref, ref, idx, (r, c ^ 1)).wait_recv()

    core_dev = (r, col(zl, x, ko))
    xr_dev, xl_dev = (r, col(zl, xr, k)), (r, col(zl, xl, k))
    zl_dev = (r, col(zlo, x, k))
    yr_dev, yl_dev = (row(zh, yr), c), (row(zh, yl), c)
    zh_dev = (row(zho, y), c)

    mine_t = own.at[:, :, pl.ds(pl.multiple_of(k * half, 128), half)]
    other_t = own.at[:, :, pl.ds(pl.multiple_of(ko * half, 128), half)]
    comps_t = comps.at[:, pl.ds(pl.multiple_of(k * half, 128), half)]
    other_dev = (t_row, t_chip + ko)
    t0 = copy(mine_t, b_out.at[c], 20, (t_row, t_chip + k))
    t2 = copy(comps_t, cb_out, 22, (t_row, t_chip + k))
    here0 = pltpu.make_async_copy(mine_t, b_out.at[c], lsem.at[1])
    here2 = pltpu.make_async_copy(comps_t, cb_out, lsem.at[2])

    @pl.when(away)
    def _():
        t0.start()

    @pl.when(jnp.logical_not(away))
    def _():
        here0.start()

    push(other_t, b_out.at[c], 21, other_dev)

    @pl.when(away)
    def _():
        t2.start()

    @pl.when(jnp.logical_not(away))
    def _():
        here2.start()

    keep = pltpu.make_async_copy(own, a_out.at[c], lsem.at[0])
    keep.start()
    push(own, a_out.at[c], 1, zl_dev)
    push(own, a_out.at[c], 2, xr_dev)
    push(own, a_out.at[c], 3, xl_dev)
    push(own, a_out.at[c], 0, core_dev)

    gram_sums(design, own, outer, acc)
    for q in range(4):
        send[q, :, 0:GRAM_ROWS] = acc[32 + 8 * q:40 + 8 * q, :]
        send[q, :, GRAM_ROWS:SUMS] = 0.5 * acc[8 * q:8 * q + 8, OFF[COMPS]:OFF[COMPS] + 128]
    wide[...] = jnp.zeros_like(wide)
    for d in range(1, 8):
        to = (r + d) % 8
        push(send.at[to % 4], recv.at[d], 31 + d, (to, c))

    t_slot = row(zh, y)

    def pair(zh_, y_):
        return b_out.at[pl.ds(2 * row(zh_, y_), 2)]

    def single(zh_, y_, h):
        return b_out.at[2 * row(zh_, y_) + h]

    @pl.when(away)
    def _():
        copy(mine_t, single(zh, y, k), 20, (t_row, t_chip + k)).wait_recv()
        copy(comps_t, cb_out, 22, (t_row, t_chip + k)).wait_recv()

    @pl.when(jnp.logical_not(away))
    def _():
        here0.wait()
        here2.wait()

    copy(other_t, single(zh, y, ko), 21, other_dev).wait_recv()
    push(pair(zh, y), pair(zh, y), 23, zh_dev)
    push(pair(zh, y), pair(zh, y), 24, yr_dev)
    push(pair(zh, y), pair(zh, y), 25, yl_dev)

    total = send[r % 4]
    for d in range(1, 8):
        arrive(recv.at[d], 31 + d)
        total = total + recv[d]
    wide[0:8, :] = total
    for q in range(SUMS // 128):
        block = wide[:, 128 * q:128 * q + 128].T
        if q < GRAM_ROWS // 128:
            gt[128 * q:128 * q + 128, :] = block
        else:
            bt[...] = block[0:WIDTH]
    solve(gt, bt, inv_s, y_s, xs)
    for q in range(2):
        coef[:, 128 * q:128 * q + 128] = xs[128 * q:128 * q + 128, :].T[0:8]
    keep_coef = pltpu.make_async_copy(coef, coef_out.at[c, y], lsem.at[3])
    keep_coef.start()
    for d in range(1, 4):
        push(coef, coef_out.at[c, y], 38 + d, (row(zh, (y + d) % 4), c))

    def slot(zl_, x_, k_):
        return a_out.at[col(zl_, x_, k_)]

    def slot_half(zl_, x_, k_, h):
        return a_out.at[col(zl_, x_, k_), h]

    arrive(slot(zlo, x, k), 1)
    push(slot(zlo, x, k), slot(zlo, x, k), 4, xr_dev)
    push(slot(zlo, x, k), slot(zlo, x, k), 5, xl_dev)
    push(slot(zlo, x, k), slot(zlo, x, k), 6, core_dev)
    arrive(slot(zl, xl, k), 2)
    push(slot_half(zl, xl, k, 0), slot_half(zl, xl, k, 0), 7, xr_dev)
    push(slot(zl, xl, k), slot(zl, xl, k), 9, core_dev)
    arrive(slot(zl, xr, k), 3)
    push(slot_half(zl, xr, k, 1), slot_half(zl, xr, k, 1), 8, xl_dev)
    push(slot(zl, xr, k), slot(zl, xr, k), 10, core_dev)

    arrive(pair(zho, y), 23)
    push(pair(zho, y), pair(zho, y), 26, yr_dev)
    push(pair(zho, y), pair(zho, y), 27, yl_dev)
    arrive(pair(zh, yl), 24)
    push(single(zh, yl, 0), single(zh, yl, 0), 28, yr_dev)
    arrive(pair(zh, yr), 25)
    push(single(zh, yr, 1), single(zh, yr, 1), 29, yl_dev)

    for d in range(1, 4):
        arrive(coef_out.at[c, (y + 4 - d) % 4], 38 + d)
    keep_coef.wait()
    for d in range(1, 16):
        push(coef_out.at[c], coef_out.at[c], 41 + d, (r, (c + d) % 16))

    arrive(slot(zlo, xl, k), 4)
    push(slot_half(zlo, xl, k, 0), slot_half(zlo, xl, k, 0), 11, xr_dev)
    push(slot(zlo, xl, k), slot(zlo, xl, k), 13, core_dev)
    arrive(slot(zlo, xr, k), 5)
    push(slot_half(zlo, xr, k, 1), slot_half(zlo, xr, k, 1), 12, xl_dev)
    push(slot(zlo, xr, k), slot(zlo, xr, k), 14, core_dev)
    arrive(pair(zho, yl), 26)
    push(single(zho, yl, 0), single(zho, yl, 0), 30, yr_dev)
    arrive(pair(zho, yr), 27)
    push(single(zho, yr, 1), single(zho, yr, 1), 31, yl_dev)

    arrive(slot_half(zl, xo, k, 0), 7)
    arrive(slot_half(zl, xo, k, 1), 8)
    push(slot(zl, xo, k), slot(zl, xo, k), 15, core_dev)
    arrive(slot_half(zlo, xo, k, 0), 11)
    arrive(slot_half(zlo, xo, k, 1), 12)
    push(slot(zlo, xo, k), slot(zlo, xo, k), 16, core_dev)

    arrive(single(zh, yo, 0), 28)
    arrive(single(zh, yo, 1), 29)
    arrive(single(zho, yo, 0), 30)
    arrive(single(zho, yo, 1), 31)
    arrive(slot(zl, x, ko), 0)
    arrive(slot(zlo, x, ko), 6)
    arrive(slot(zl, xl, ko), 9)
    arrive(slot(zl, xr, ko), 10)
    arrive(slot(zlo, xl, ko), 13)
    arrive(slot(zlo, xr, ko), 14)
    arrive(slot(zl, xo, ko), 15)
    arrive(slot(zlo, xo, ko), 16)
    for d in range(1, 16):
        arrive(coef_out.at[(c + 16 - d) % 16], 41 + d)

    keep.wait()

    @pl.when(away)
    def _():
        t0.wait_send()
        t2.wait_send()

    for one in sent:
        one.wait_send()


def gather(dosage, present, comps):
    markers, people = dosage.shape
    half = people // 2
    any_space = pl.BlockSpec(memory_space=pl.ANY)
    vmem = pl.BlockSpec(memory_space=pltpu.VMEM)
    return pl.pallas_call(
        gather_kernel,
        out_shape=(
            jax.ShapeDtypeStruct((16, 2, markers, people), BF16),
            jax.ShapeDtypeStruct((16, 2, markers, half), BF16),
            jax.ShapeDtypeStruct((COMPS, half), F32),
            jax.ShapeDtypeStruct((16, 4, 8, 256), F32),
        ),
        in_specs=[vmem] * 3,
        out_specs=(any_space,) * 4,
        scratch_shapes=[
            pltpu.VMEM((2, markers, people), BF16),
            pltpu.VMEM((WIDTH, people), F32),
            pltpu.VMEM((GRAM_ROWS, CHUNK), F32),
            pltpu.VMEM((64, GRAM_ROWS), F32),
            pltpu.VMEM((4, 8, SUMS), F32),
            pltpu.VMEM((8, 8, SUMS), F32),
            pltpu.VMEM((128, SUMS), F32),
            pltpu.VMEM((GRAM_ROWS, 128), F32),
            pltpu.VMEM((WIDTH, 128), F32),
            pltpu.VMEM((COMPS + 1, 8, 128), F32),
            pltpu.VMEM((COMPS + 1, 8, 128), F32),
            pltpu.VMEM((256, 128), F32),
            pltpu.VMEM((8, 256), F32),
            pltpu.SemaphoreType.DMA((60,)),
            pltpu.SemaphoreType.DMA((60,)),
            pltpu.SemaphoreType.DMA((4,)),
        ],
        compiler_params=pltpu.CompilerParams(collective_id=0, has_side_effects=True),
        name="gather_fit",
    )(dosage, present, comps)


def form(raw, comps, coef, stack, resid, sdev):
    width = comps.shape[1]
    hi, mid, low = split3(comps)
    sub = lax.broadcasted_iota(jnp.int32, (8, width), 0)
    ones = jnp.where(sub == 0, 1.0, 0.0).astype(F32)
    zeros = jnp.zeros((8, width), F32)
    for t, part in enumerate((hi, mid, low, hi, mid, hi)):
        stack[WIDTH * t:WIDTH * t + COMPS, :] = part
        stack[WIDTH * t + COMPS:WIDTH * (t + 1), :] = ones if part is hi else zeros
    stack[6 * WIDTH:, :] = jnp.zeros((256 - 6 * WIDTH, width), F32)
    twice = jnp.dot(coef, stack[...].astype(BF16), preferred_element_type=F32)
    twice = jnp.clip(twice, 0.02, 1.98)
    counts = raw[:, 0].reshape(512, width)
    seen = raw[:, 1].reshape(512, width)
    resid[...] = (counts.astype(F32) - twice).astype(BF16) * seen
    spread = twice * (2.0 - twice)
    sdev[...] = (spread * lax.rsqrt(spread)).astype(BF16) * seen


def ratio_kernel(a_ref, b_ref, ca_ref, cb_ref, coef_ref, out_ref,
                 rb, sb, ra, sa, stack_a, stack_b):
    coef = coef_ref[...].astype(BF16)

    @pl.when(pl.program_id(0) == 0)
    def _():
        for h in range(3):
            at = slice(512 * h, 512 * h + 512)
            form(b_ref[:, :, :, at], cb_ref[:, at], coef, stack_b, rb.at[:, at], sb.at[:, at])

    form(a_ref[...], ca_ref[...], coef, stack_a, ra, sa)
    contract = (((0,), (0,)), ((), ()))
    numer = lax.dot_general(ra[...], rb[...], contract, preferred_element_type=F32)
    denom = lax.dot_general(sa[...], sb[...], contract, preferred_element_type=F32)
    out_ref[...] = numer / denom


def ratio(a_raw, b_raw, comps, comps_b, coef):
    people = comps.shape[1]
    half = people // 2
    tile = 256
    whole = lambda shape: pl.BlockSpec(shape, lambda i: (0,) * len(shape), pipeline_mode=pl.Buffered(1))
    return pl.pallas_call(
        ratio_kernel,
        out_shape=jax.ShapeDtypeStruct((people, half), F32),
        grid=(people // tile,),
        in_specs=[
            pl.BlockSpec((16, 2, 32, tile), lambda i: (0, 0, 0, i)),
            whole((16, 2, 32, half)),
            pl.BlockSpec((COMPS, tile), lambda i: (0, i)),
            whole((COMPS, half)),
            whole((512, 256)),
        ],
        out_specs=pl.BlockSpec((tile, half), lambda i: (i, 0)),
        scratch_shapes=[
            pltpu.VMEM((512, half), BF16),
            pltpu.VMEM((512, half), BF16),
            pltpu.VMEM((512, tile), BF16),
            pltpu.VMEM((512, tile), BF16),
            pltpu.VMEM((256, tile), F32),
            pltpu.VMEM((256, 512), F32),
        ],
        name="form_ratio",
    )(a_raw, b_raw, comps, comps_b, coef)


def per_device(dosage, present, comps):
    a_raw, b_raw, comps_b, coef = gather(dosage, present, comps)
    return ratio(a_raw, b_raw, comps, comps_b, coef.reshape(512, 256))


def solution(mesh):
    placed = (P("cols", "rows"), P("cols", "rows"), P(None, "rows"))
    return jax.shard_map(
        per_device, mesh=mesh, in_specs=placed, out_specs=P("rows", "cols"), check_vma=False
    )
```

time: 340 us -> 93.3 us (0.27); the launches traced: 335 us -> 92.8 us
  waiting for transfers between devices: 188 us -> 0 us
  Pallas kernels: 0 us -> 92.8 us
  matrix products: 41.3 us -> 0 us
  other arithmetic: 37.7 us -> 0 us
  blocking collectives: 37.2 us -> 0 us
  local copies, waits for them, and re-layouts: 16.1 us -> 0 us
  between operations: 14.6 us -> 0.01 us
    psum x2 -> x0, waiting for transfers between devices: 142 us -> none  [the longest x1 96.2 us: broadcast(): return lax.psum(block, axis)]
    pallas_call x0 -> x2, Pallas kernels: none -> 92.8 us  [the longest x1 71.4 us: gather(): pl.pallas_call(gather_kernel, out_shape=(jax.ShapeDtypeStruct((16, 2, mar...]
    all_gather x1 -> x0, waiting for transfers between devices: 46.4 us -> none  [per_device(): full_rows = lax.all_gather(panel, 'cols', axis=1, tiled=True)]
    dot_general x5 -> x0, matrix products: 41.3 us -> none  [the longest x1 14.2 us: per_device(): jnp.dot(outer_rows, observed.T, precision=lax.Precision.HIGHEST, preferre...]
    psum x1 -> x0, blocking collectives: 37.2 us -> none  [per_device(): gram_flat, moment = lax.psum((gram_part, moment_part), 'rows')]
    mul x1 -> x0, local copies, waits for them, and re-layouts: 10.5 us -> none  [per_device(): design[:, None, :] * design[None, :, :]]
    unnamed x32 -> x0, other arithmetic: 10.3 us -> none
    mul x1 -> x0, other arithmetic: 8.02 us -> none  [per_device(): design[:, None, :] * design[None, :, :]]
  transfers between devices with their start and end apart: 3 -> 0, of which waited for: 3 -> 0; matrix products, arithmetic and copies ran while one was open for 0% -> 0% of each run, Pallas kernels for 0% -> 0%
where the time goes in v1:
time: 93.3 us; the launch traced here: 92.8 us
  Pallas kernels  92.8 us (99%)
    pallas_call x1, Pallas kernels, gather(): pl.pallas_call(gather_kernel, out_shape=(jax.ShapeDtypeStruct((16, 2, mar...  71.4 us
    pallas_call x1, Pallas kernels, ratio(): pl.pallas_call(ratio_kernel, out_shape=jax.ShapeDtypeStruct((people, half...  21.3 us

profile of v1, /device:TPU:1, one launch (start us, length us, event | category | flops | bytes accessed | tf_op | source)
XLA Modules:
  0.0 92.8 jit_solution(14804332093011054491)
XLA Ops:
  0.0 71.4 %gather_fit.1 = (bf16[16,2,32,3072]{3,2,1,0:T(8,128)(2,1)}, bf16[16,2,32,1536]{3,2,1,0:T(8,128)(2,1)}, f32[32,1536]{1,0:T(8,128)}, f32[16,4,8,256]{3,2,1,0:T(8,128)}) custom-call(s32[32,3072]{1,0:T(8,128)} %dosage.1, s32[32,3072]{1,0:T(8,128)} %present.1, f32[32,3072]{1,0:T(8,128)} %ca_ref.1), custom_call_target="tpu_custom_call" | custom-call | tf_op jit(solution)/shard_map/gather_fit/pallas_call | solution.py:328
  71.5 21.3 %form_ratio.1 = f32[3072,1536]{1,0:T(8,128)} custom-call(bf16[16,2,32,3072]{3,2,1,0:T(8,128)(2,1)} %get-tuple-element.9.a_ref, bf16[16,2,32,1536]{3,2,1,0:T(8,128)(2,1)} %get-tuple-element.10.b_ref, f32[32,3072]{1,0:T(8,128)} %ca_ref.1, f32[32,1536]{1,0:T(8,128)} %get-tuple-element.11.cb_ref, f32[512,256]{1,0:T(8,128)} %bitcast.1), custom_call_target="tpu_custom_call" | custom-call | tf_op jit(solution)/shard_map/form_ratio/pallas_call | solution.py:402

commit v2 on v1

v2 whole, which is shorter than its diff:
```python
import functools

import jax
import jax.numpy as jnp
from jax import lax
from jax.experimental import pallas as pl
from jax.experimental.pallas import tpu as pltpu
from jax.sharding import PartitionSpec as P

F32 = jnp.float32
BF16 = jnp.bfloat16
MESH = pl.DeviceIdType.MESH

COMPS = 32
WIDTH = 40
CHUNK = 512
OFF = []
for _i in range(COMPS + 1):
    OFF.append(sum(8 * (k // 8 + 1) for k in range(_i)))
GRAM_ROWS = 768
SUMS = 896


def rows_of(i):
    return 8 * (i // 8 + 1)


def split3(value):
    hi = value.astype(BF16).astype(F32)
    rest = value - hi
    mid = rest.astype(BF16).astype(F32)
    low = (rest - mid).astype(BF16).astype(F32)
    return hi, mid, low


def gram_sums(design, own, outer, acc):
    people = design.shape[1]
    acc[...] = jnp.zeros_like(acc)
    outer[OFF[COMPS] + WIDTH:, :] = jnp.zeros((GRAM_ROWS - OFF[COMPS] - WIDTH, CHUNK), F32)

    def chunk(step, carry):
        at = pl.ds(pl.multiple_of(step * CHUNK, CHUNK), CHUNK)
        for i in range(COMPS + 1):
            n = rows_of(i)
            outer[OFF[i]:OFF[i] + n, :] = design[0:n, at] * design[i:i + 1, at]
        left = own[:, :, at].reshape(64, CHUNK)
        value = outer[...]
        total = acc[...]
        for _ in range(3):
            piece = value.astype(BF16)
            total += lax.dot_general(
                left, piece, (((1,), (1,)), ((), ())), preferred_element_type=F32
            )
            value = value - piece.astype(F32)
        acc[...] = total
        return carry

    lax.fori_loop(0, people // CHUNK, chunk, 0)


def solve(gt, bt, inv_s, y_s, xs):
    for j in range(COMPS, -1, -1):
        n = rows_of(j)
        base = OFF[j]
        pivot = gt[pl.ds(base + j, 8, stride=0), :]
        inv = lax.rsqrt(pivot)
        inv = inv * (1.5 - 0.5 * pivot * inv * inv)
        inv_s[j] = inv
        column = [gt[base + 8 * q:base + 8 * q + 8, :] * inv for q in range(n // 8)]
        for q in range(n // 8):
            gt[base + 8 * q:base + 8 * q + 8, :] = column[q]
        y = bt[pl.ds(j, 8, stride=0), :] * inv
        y_s[j] = y
        for q in range(n // 8):
            bt[8 * q:8 * q + 8, :] = bt[8 * q:8 * q + 8, :] - y * column[q]
        for i in range(j - 1, -1, -1):
            factor = gt[pl.ds(base + i, 8, stride=0), :]
            for q in range(i // 8 + 1):
                lo = OFF[i] + 8 * q
                gt[lo:lo + 8, :] = gt[lo:lo + 8, :] - factor * column[q]
    sub = lax.broadcasted_iota(jnp.int32, (8, 128), 0)
    x = [jnp.zeros((8, 128), F32) for _ in range(WIDTH // 8)]
    for j in range(COMPS + 1):
        value = y_s[j]
        if j > 0:
            total = gt[OFF[j]:OFF[j] + 8, :] * x[0]
            for q in range(1, rows_of(j) // 8):
                total += gt[OFF[j] + 8 * q:OFF[j] + 8 * q + 8, :] * x[q]
            value = value - jnp.sum(total, axis=0, keepdims=True)
        value = value * inv_s[j]
        x[j // 8] = jnp.where(sub == j % 8, value, x[j // 8])
    twice = jnp.concatenate(x, axis=0) * 2.0
    for t, part in enumerate(split3(twice)):
        xs[WIDTH * t:WIDTH * t + WIDTH, :] = part
    xs[3 * WIDTH:, :] = jnp.zeros((128 - 3 * WIDTH, 128), F32)


def gather_kernel(dosage, present, comps, a_out, b_out, cb_out, coef_out,
                  own, relay, relay_z, relay_c, design, outer, acc, send, recv, wide, gt, bt,
                  inv_s, y_s, xs, coef, ssem, rsem, lsem):
    r = lax.axis_index("rows")
    c = lax.axis_index("cols")
    zh, y = r // 4, r % 4
    zl, x, k = c // 8, (c // 2) % 4, c % 2
    people = dosage.shape[1]
    half = people // 2

    def col(zl_, x_, k_):
        return zl_ * 8 + x_ * 2 + k_

    def row(zh_, y_):
        return zh_ * 4 + y_

    xr, xl, xo = (x + 1) % 4, (x + 3) % 4, (x + 2) % 4
    yr, yl, yo = (y + 1) % 4, (y + 3) % 4, (y + 2) % 4
    zlo, zho, ko = 1 - zl, 1 - zh, 1 - k
    turn = [[(x - y + 4 + 2 * p + q) % 4 for q in range(2)] for p in range(2)]
    turn_mine = [(x - y + 4 + 2 * p + k) % 4 for p in range(2)]
    turn_other = [(x - y + 4 + 2 * p + ko) % 4 for p in range(2)]
    swapped = zh != zl

    barrier = pltpu.get_barrier_semaphore()
    for d in range(1, 8):
        pl.semaphore_signal(barrier, inc=1, device_id=((r + d) % 8, c), device_id_type=MESH)
    for d in range(1, 16):
        pl.semaphore_signal(barrier, inc=1, device_id=(r, (c + d) % 16), device_id_type=MESH)

    pl.semaphore_signal(
        barrier, inc=1, device_id=(row(zho, y), col(zlo, x, k)), device_id_type=MESH
    )

    @pl.when(swapped)
    def _():
        for q in range(8):
            pl.semaphore_signal(
                barrier, inc=1, device_id=(row(zl, y), zh * 8 + q), device_id_type=MESH
            )

    seen = present[...].astype(F32)
    own[0] = (dosage[...].astype(F32) * seen).astype(BF16)
    own[1] = seen.astype(BF16)
    design[0:COMPS, :] = comps[...]
    sub = lax.broadcasted_iota(jnp.int32, (8, people), 0)
    design[COMPS:WIDTH, :] = jnp.where(sub == 0, 1.0, 0.0).astype(F32)

    pl.semaphore_wait(barrier, jnp.where(swapped, 31, 23))

    sent = []
    names = {}

    def copy(src, dst, name, dev):
        idx = names.setdefault(name, len(names))
        return pltpu.make_async_remote_copy(
            src_ref=src, dst_ref=dst, send_sem=ssem.at[idx], recv_sem=rsem.at[idx],
            device_id=dev, device_id_type=MESH,
        )

    def push(src, dst, name, dev):
        one = copy(src, dst, name, dev)
        one.start()
        sent.append(one.wait_send)

    def pass_on(ref, name, dev):
        push(ref, ref, name, dev)

    core_dev = (r, col(zl, x, ko))

    def arrive(ref, name):
        copy(ref, ref, name, core_dev).wait_recv()

    def push_or_keep(here, src, dst, name, dev):
        one = copy(src, dst, name, dev)
        local = pltpu.make_async_copy(src, dst, lsem.at[names[name]])

        @pl.when(here)
        def _():
            local.start()

        @pl.when(jnp.logical_not(here))
        def _():
            one.start()

        def finish():
            @pl.when(jnp.logical_not(here))
            def _():
                one.wait_send()

        sent.append(finish)

    def arrive_or_keep(here, ref, name):
        one = copy(ref, ref, name, core_dev)
        local = pltpu.make_async_copy(ref, ref, lsem.at[names[name]])

        @pl.when(here)
        def _():
            local.wait()

        @pl.when(jnp.logical_not(here))
        def _():
            one.wait_recv()

    xr_dev, xl_dev = (r, col(zl, xr, k)), (r, col(zl, xl, k))
    zl_dev = (r, col(zlo, x, k))
    yr_dev, yl_dev = (row(zh, yr), c), (row(zh, yl), c)
    crosses = [zl == 1, zl == 0]
    z_dev = [(row(jnp.where(crosses[p], zho, zh), y), col(zlo, x, k)) for p in range(2)]
    zh_from = [jnp.where(crosses[1 - p], zho, zh) for p in range(2)]

    def a_slot(zl_, x_, k_, p=None):
        ref = a_out.at[col(zl_, x_, k_)]
        return ref if p is None else ref.at[p]

    def piece(ref, at):
        return ref.at[pl.ds(pl.multiple_of(8 * at, 8), 8)]

    def people_half(ref, q):
        return ref.at[:, pl.ds(pl.multiple_of(q * half, 128), half)]

    def leg1(p, q):
        push_or_keep(turn[p][q] == y, people_half(own.at[p], q), relay.at[p, q],
                     f"leg1_{p}{q}", (row(zh, turn[p][q]), c))

    leg1(0, 0)
    leg1(0, 1)
    push(own.at[0], a_slot(zl, x, k, 0), "own_xr0", xr_dev)
    push(own.at[0], a_slot(zl, x, k, 0), "own_xl0", xl_dev)
    push(own.at[0], a_slot(zl, x, k, 0), "own_zl0", zl_dev)
    leg1(1, 0)
    leg1(1, 1)
    push_or_keep(turn_mine[0] == y, people_half(piece(comps, turn_mine[0]), k), relay_c,
                 "leg1_c", (row(zh, turn_mine[0]), c))
    push(own.at[1], a_slot(zl, x, k, 1), "own_zl1", zl_dev)
    push(own, a_slot(zl, x, k), "own_core", core_dev)
    keep = pltpu.make_async_copy(own, a_out.at[c], lsem.at[127])
    keep.start()

    gram_sums(design, own, outer, acc)
    for q in range(4):
        send[q, :, 0:GRAM_ROWS] = acc[32 + 8 * q:40 + 8 * q, :]
        send[q, :, GRAM_ROWS:SUMS] = 0.5 * acc[8 * q:8 * q + 8, OFF[COMPS]:OFF[COMPS] + 128]
    wide[...] = jnp.zeros_like(wide)
    for d in range(1, 8):
        to = (r + d) % 8
        push(send.at[to % 4], recv.at[d], ("rs", d), (to, c))

    def home(p):
        return jnp.logical_and(zh == zl, turn_mine[p] == x)

    def leg2(p):
        chip_row = row(zl, y)
        for q in range(2):
            arrive_or_keep(turn[p][q] == y, relay.at[p, q], f"leg1_{p}{q}")
        push_or_keep(home(p), relay.at[p, k], b_out.at[p, c],
                     f"leg2_{p}_same", (chip_row, col(zh, turn_mine[p], k)))
        push(relay.at[p, ko], b_out.at[p, c],
             f"leg2_{p}_other", (chip_row, col(zh, turn_other[p], ko)))

    def leg2_c():
        arrive_or_keep(turn_mine[0] == y, relay_c, "leg1_c")
        push_or_keep(home(0), relay_c, piece(cb_out, y),
                     "leg2_c_same", (row(zl, y), col(zh, turn_mine[0], k)))

    def b_one(p, zh_, y_, k_):
        return b_out.at[p, 2 * row(zh_, (x + y_ + 8 - 2 * p - k) % 4) + k_]

    leg2(0)
    leg2(1)
    push(own.at[1], a_slot(zl, x, k, 1), "own_xr1", xr_dev)
    push(own.at[1], a_slot(zl, x, k, 1), "own_xl1", xl_dev)
    leg2_c()

    for p in range(2):
        arrive(a_slot(zlo, x, k, p), f"own_zl{p}")
        pass_on(a_slot(zlo, x, k, p), f"zl_xr{p}", xr_dev)
        pass_on(a_slot(zlo, x, k, p), f"zl_xl{p}", xl_dev)
    pass_on(a_slot(zlo, x, k), "zl_core", core_dev)

    core_of = [k, ko]

    def start_column(p, e):
        ref = b_one(p, zh, y, core_of[e])
        if e == 0:
            arrive_or_keep(home(p), ref, f"leg2_{p}_same")
        else:
            arrive(ref, f"leg2_{p}_other")
        push(ref, relay_z.at[p, e], f"b_mid{p}{e}", z_dev[p])
        pass_on(ref, f"b_yr{p}{e}", yr_dev)
        pass_on(ref, f"b_yl{p}{e}", yl_dev)

    def relay_column(p, e):
        arrive(relay_z.at[p, e], f"b_mid{p}{e}")
        push(relay_z.at[p, e], b_one(p, zh_from[p], y, core_of[e]), f"b_zh{p}{e}", z_dev[p])

    def turn_column(p, e):
        ref = b_one(p, zho, y, core_of[e])
        arrive(ref, f"b_zh{p}{e}")
        pass_on(ref, f"bz_yr{p}{e}", yr_dev)
        pass_on(ref, f"bz_yl{p}{e}", yl_dev)

    def far_column(p, e, zh_, tag):
        right, left = b_one(p, zh_, yl, core_of[e]), b_one(p, zh_, yr, core_of[e])
        arrive(right, f"{tag}_yr{p}{e}")
        arrive(left, f"{tag}_yl{p}{e}")
        if p == 0:
            pass_on(right, f"{tag}_far{p}{e}", yr_dev)
        else:
            pass_on(left, f"{tag}_far{p}{e}", yl_dev)

    parts = [(p, e) for p in range(2) for e in range(2)]
    for p, e in parts:
        start_column(p, e)
    for p, e in parts:
        relay_column(p, e)
    arrive_or_keep(home(0), piece(cb_out, y), "leg2_c_same")
    pass_on(piece(cb_out, y), "c_yr", yr_dev)
    pass_on(piece(cb_out, y), "c_yl", yl_dev)

    total = send[r % 4]
    for d in range(1, 8):
        arrive(recv.at[d], ("rs", d))
        total = total + recv[d]
    wide[0:8, :] = total
    for q in range(SUMS // 128):
        block = wide[:, 128 * q:128 * q + 128].T
        if q < GRAM_ROWS // 128:
            gt[128 * q:128 * q + 128, :] = block
        else:
            bt[...] = block[0:WIDTH]
    solve(gt, bt, inv_s, y_s, xs)
    coef[...] = xs[...].T[0:8]
    keep_coef = pltpu.make_async_copy(coef, coef_out.at[c, y], lsem.at[126])
    keep_coef.start()
    for d in range(1, 4):
        push(coef, coef_out.at[c, y], ("cag", d), (row(zh, (y + d) % 4), c))

    for p in range(2):
        arrive(a_slot(zl, xl, k, p), f"own_xr{p}")
        arrive(a_slot(zl, xr, k, p), f"own_xl{p}")
        if p == 0:
            pass_on(a_slot(zl, xl, k, 0), "far_xr", xr_dev)
        else:
            pass_on(a_slot(zl, xr, k, 1), "far_xl", xl_dev)
    pass_on(a_slot(zl, xl, k), "xl_core", core_dev)
    pass_on(a_slot(zl, xr, k), "xr_core", core_dev)

    for p, e in parts:
        far_column(p, e, zh, "b")
    for p, e in parts:
        turn_column(p, e)
    arrive(piece(cb_out, yl), "c_yr")
    pass_on(piece(cb_out, yl), "c_far", yr_dev)
    arrive(piece(cb_out, yr), "c_yl")

    for d in range(1, 4):
        arrive(coef_out.at[c, (y + 4 - d) % 4], ("cag", d))
    keep_coef.wait()
    for d in range(1, 16):
        push(coef_out.at[c], coef_out.at[c], ("rag", d), (r, (c + d) % 16))

    for p in range(2):
        arrive(a_slot(zlo, xl, k, p), f"zl_xr{p}")
        arrive(a_slot(zlo, xr, k, p), f"zl_xl{p}")
        if p == 0:
            pass_on(a_slot(zlo, xl, k, 0), "zfar_xr", xr_dev)
        else:
            pass_on(a_slot(zlo, xr, k, 1), "zfar_xl", xl_dev)
    pass_on(a_slot(zlo, xl, k), "zxl_core", core_dev)
    pass_on(a_slot(zlo, xr, k), "zxr_core", core_dev)
    for p, e in parts:
        far_column(p, e, zho, "bz")

    arrive(a_slot(zl, xo, k, 0), "far_xr")
    arrive(a_slot(zl, xo, k, 1), "far_xl")
    pass_on(a_slot(zl, xo, k), "far_core", core_dev)
    for p, e in parts:
        arrive(b_one(p, zh, yo, core_of[e]), f"b_far{p}{e}")
    arrive(piece(cb_out, yo), "c_far")
    arrive(a_slot(zlo, xo, k, 0), "zfar_xr")
    arrive(a_slot(zlo, xo, k, 1), "zfar_xl")
    pass_on(a_slot(zlo, xo, k), "zfar_core", core_dev)
    for p, e in parts:
        arrive(b_one(p, zho, yo, core_of[e]), f"bz_far{p}{e}")

    arrive(a_slot(zl, x, ko), "own_core")
    arrive(a_slot(zlo, x, ko), "zl_core")
    arrive(a_slot(zl, xl, ko), "xl_core")
    arrive(a_slot(zl, xr, ko), "xr_core")
    arrive(a_slot(zlo, xl, ko), "zxl_core")
    arrive(a_slot(zlo, xr, ko), "zxr_core")
    arrive(a_slot(zl, xo, ko), "far_core")
    arrive(a_slot(zlo, xo, ko), "zfar_core")
    for d in range(1, 16):
        arrive(coef_out.at[(c + 16 - d) % 16], ("rag", d))
    keep.wait()
    for finish in sent:
        finish()


def gather(dosage, present, comps):
    markers, people = dosage.shape
    half = people // 2
    any_space = pl.BlockSpec(memory_space=pl.ANY)
    vmem = pl.BlockSpec(memory_space=pltpu.VMEM)
    return pl.pallas_call(
        gather_kernel,
        out_shape=(
            jax.ShapeDtypeStruct((16, 2, markers, people), BF16),
            jax.ShapeDtypeStruct((2, 16, markers, half), BF16),
            jax.ShapeDtypeStruct((COMPS, half), F32),
            jax.ShapeDtypeStruct((16, 4, 8, 128), F32),
        ),
        in_specs=[vmem] * 3,
        out_specs=(any_space,) * 4,
        scratch_shapes=[
            pltpu.VMEM((2, markers, people), BF16),
            pltpu.VMEM((2, 2, markers, half), BF16),
            pltpu.VMEM((2, 2, markers, half), BF16),
            pltpu.VMEM((8, half), F32),
            pltpu.VMEM((WIDTH, people), F32),
            pltpu.VMEM((GRAM_ROWS, CHUNK), F32),
            pltpu.VMEM((64, GRAM_ROWS), F32),
            pltpu.VMEM((4, 8, SUMS), F32),
            pltpu.VMEM((8, 8, SUMS), F32),
            pltpu.VMEM((128, SUMS), F32),
            pltpu.VMEM((GRAM_ROWS, 128), F32),
            pltpu.VMEM((WIDTH, 128), F32),
            pltpu.VMEM((COMPS + 1, 8, 128), F32),
            pltpu.VMEM((COMPS + 1, 8, 128), F32),
            pltpu.VMEM((128, 128), F32),
            pltpu.VMEM((8, 128), F32),
            pltpu.SemaphoreType.DMA((128,)),
            pltpu.SemaphoreType.DMA((128,)),
            pltpu.SemaphoreType.DMA((128,)),
        ],
        compiler_params=pltpu.CompilerParams(collective_id=0, has_side_effects=True),
        name="gather_fit",
    )(dosage, present, comps)


def form(counts, seen, comps, coef, stack, resid, sdev):
    width = comps.shape[1]
    hi, mid, low = split3(comps)
    sub = lax.broadcasted_iota(jnp.int32, (8, width), 0)
    ones = jnp.where(sub == 0, 1.0, 0.0).astype(F32)
    zeros = jnp.zeros((8, width), F32)
    stack[...] = jnp.zeros_like(stack)
    for group, parts in ((0, (hi, hi, hi)), (128, (mid, mid)), (256, (low,))):
        for t, part in enumerate(parts):
            at = group + WIDTH * t
            stack[at:at + COMPS, :] = part
            stack[at + COMPS:at + WIDTH, :] = ones if part is hi else zeros
    right = stack[...].astype(BF16)
    twice = jnp.dot(jnp.concatenate([coef, coef], axis=1), right[0:256], preferred_element_type=F32)
    twice += jnp.dot(coef, right[256:384], preferred_element_type=F32)
    twice = jnp.clip(twice, 0.02, 1.98)
    resid[...] = (counts.astype(F32) - twice).astype(BF16) * seen
    spread = twice * (2.0 - twice)
    sdev[...] = (spread * lax.rsqrt(spread)).astype(BF16) * seen


def ratio_kernel(a_ref, b_ref, ca_ref, cb_ref, coef_ref, out_ref,
                 rb, sb, ra, sa, stack_a, stack_b):
    coef = coef_ref[...].astype(BF16)

    @pl.when(pl.program_id(0) == 0)
    def _():
        for h in range(3):
            at = slice(512 * h, 512 * h + 512)
            form(b_ref[0, :, :, at].reshape(512, 512), b_ref[1, :, :, at].reshape(512, 512),
                 cb_ref[:, at], coef, stack_b, rb.at[:, at], sb.at[:, at])

    tile = ra.shape[1]
    form(a_ref[:, 0].reshape(512, tile), a_ref[:, 1].reshape(512, tile),
         ca_ref[...], coef, stack_a, ra, sa)
    contract = (((0,), (0,)), ((), ()))
    numer = lax.dot_general(ra[...], rb[...], contract, preferred_element_type=F32)
    denom = lax.dot_general(sa[...], sb[...], contract, preferred_element_type=F32)
    out_ref[...] = numer / denom


def ratio(a_raw, b_raw, comps, comps_b, coef):
    people = comps.shape[1]
    half = people // 2
    tile = 256
    whole = lambda shape: pl.BlockSpec(shape, lambda i: (0,) * len(shape), pipeline_mode=pl.Buffered(1))
    return pl.pallas_call(
        ratio_kernel,
        out_shape=jax.ShapeDtypeStruct((people, half), F32),
        grid=(people // tile,),
        in_specs=[
            pl.BlockSpec((16, 2, 32, tile), lambda i: (0, 0, 0, i)),
            whole((2, 16, 32, half)),
            pl.BlockSpec((COMPS, tile), lambda i: (0, i)),
            whole((COMPS, half)),
            whole((512, 128)),
        ],
        out_specs=pl.BlockSpec((tile, half), lambda i: (i, 0)),
        scratch_shapes=[
            pltpu.VMEM((512, half), BF16),
            pltpu.VMEM((512, half), BF16),
            pltpu.VMEM((512, tile), BF16),
            pltpu.VMEM((512, tile), BF16),
            pltpu.VMEM((384, tile), F32),
            pltpu.VMEM((384, 512), F32),
        ],
        name="form_ratio",
    )(a_raw, b_raw, comps, comps_b, coef)


def per_device(dosage, present, comps):
    a_raw, b_raw, comps_b, coef = gather(dosage, present, comps)
    return ratio(a_raw, b_raw, comps, comps_b, coef.reshape(512, 128))


def solution(mesh):
    placed = (P("cols", "rows"), P("cols", "rows"), P(None, "rows"))
    return jax.shard_map(
        per_device, mesh=mesh, in_specs=placed, out_specs=P("rows", "cols"), check_vma=False
    )
```

time: 93.3 us -> 80.7 us (0.86)
  Pallas kernels: 92.8 us -> 80.4 us
    pallas_call x1, Pallas kernels: 71.4 us -> 57.2 us  [gather(): pl.pallas_call(gather_kernel, out_shape=(jax.ShapeDtypeStruct((16, 2, mar...]
    pallas_call x1, Pallas kernels: 21.3 us -> 23.2 us  [ratio(): pl.pallas_call(ratio_kernel, out_shape=jax.ShapeDtypeStruct((people, half...]
where the time goes in v2:
time: 80.7 us; the launch traced here: 80.4 us
  Pallas kernels  80.4 us (100%)
    pallas_call x1, Pallas kernels, gather(): pl.pallas_call(gather_kernel, out_shape=(jax.ShapeDtypeStruct((16, 2, mar...  57.2 us
    pallas_call x1, Pallas kernels, ratio(): pl.pallas_call(ratio_kernel, out_shape=jax.ShapeDtypeStruct((people, half...  23.2 us

profile of v2, /device:TPU:1, one launch (start us, length us, event | category | flops | bytes accessed | tf_op | source)
XLA Modules:
  0.0 80.4 jit_solution(14780345477967461615)
XLA Ops:
  0.0 57.2 %gather_fit.1 = (bf16[16,2,32,3072]{3,2,1,0:T(8,128)(2,1)}, bf16[2,16,32,1536]{3,2,1,0:T(8,128)(2,1)}, f32[32,1536]{1,0:T(8,128)}, f32[16,4,8,128]{3,2,1,0:T(8,128)}) custom-call(s32[32,3072]{1,0:T(8,128)} %dosage.1, s32[32,3072]{1,0:T(8,128)} %present.1, f32[32,3072]{1,0:T(8,128)} %ca_ref.1), custom_call_target="tpu_custom_call" | custom-call | tf_op jit(solution)/shard_map/gather_fit/pallas_call | solution.py:404
  57.2 23.2 %form_ratio.1 = f32[3072,1536]{1,0:T(8,128)} custom-call(bf16[16,2,32,3072]{3,2,1,0:T(8,128)(2,1)} %get-tuple-element.9.a_ref, bf16[2,16,32,1536]{3,2,1,0:T(8,128)(2,1)} %get-tuple-element.10.b_ref, f32[32,3072]{1,0:T(8,128)} %ca_ref.1, f32[32,1536]{1,0:T(8,128)} %get-tuple-element.11.cb_ref, f32[512,128]{1,0:T(8,128)} %bitcast.1), custom_call_target="tpu_custom_call" | custom-call | tf_op jit(solution)/shard_map/form_ratio/pallas_call | solution.py:486

commit v3 on v2

--- a/solution.py
+++ b/solution.py
@@ -443,68 +443,95 @@
     sub = lax.broadcasted_iota(jnp.int32, (8, width), 0)
     ones = jnp.where(sub == 0, 1.0, 0.0).astype(F32)
     zeros = jnp.zeros((8, width), F32)
-    stack[...] = jnp.zeros_like(stack)
-    for group, parts in ((0, (hi, hi, hi)), (128, (mid, mid)), (256, (low,))):
-        for t, part in enumerate(parts):
-            at = group + WIDTH * t
-            stack[at:at + COMPS, :] = part
-            stack[at + COMPS:at + WIDTH, :] = ones if part is hi else zeros
-    right = stack[...].astype(BF16)
-    twice = jnp.dot(jnp.concatenate([coef, coef], axis=1), right[0:256], preferred_element_type=F32)
-    twice += jnp.dot(coef, right[256:384], preferred_element_type=F32)
+    for at, part in ((0, hi), (40, hi), (80, hi), (128, mid), (168, mid), (208, low)):
+        stack[at:at + COMPS, :] = part
+        stack[at + COMPS:at + WIDTH, :] = ones if part is hi else zeros
+    for at in (120, 248):
+        stack[at:at + 8, :] = zeros
+    twice = jnp.dot(coef, stack[...].astype(BF16), preferred_element_type=F32)
     twice = jnp.clip(twice, 0.02, 1.98)
     resid[...] = (counts.astype(F32) - twice).astype(BF16) * seen
     spread = twice * (2.0 - twice)
     sdev[...] = (spread * lax.rsqrt(spread)).astype(BF16) * seen
 
 
-def ratio_kernel(a_ref, b_ref, ca_ref, cb_ref, coef_ref, out_ref,
-                 rb, sb, ra, sa, stack_a, stack_b):
-    coef = coef_ref[...].astype(BF16)
+def ratio_kernel(steps, a0_ref, a1_ref, a2_ref, b_ref, c0_ref, c1_ref, c2_ref, cb_ref, coef_ref, out_ref,
+                 left, rb, sb, ra0, sa0, ra1, sa1, stack, stack_b):
+    tile = ra0.shape[1]
+    half = rb.shape[1]
+    piece = 256
+
+    def form_a(a_ref, c_ref, ra, sa, h):
+        at = slice(piece * h, piece * h + piece)
+        form(a_ref[:, 0, :, at].reshape(512, piece), a_ref[:, 1, :, at].reshape(512, piece),
+             c_ref[:, at], left[...], stack.at[h], ra.at[:, at], sa.at[:, at])
 
     @pl.when(pl.program_id(0) == 0)
     def _():
-        for h in range(3):
+        base = coef_ref[...]
+        lane = lax.broadcasted_iota(jnp.int32, base.shape, 1)
+        left[:, 0:128] = base.astype(BF16)
+        left[:, 128:256] = jnp.where(lane < 2 * WIDTH, base, pltpu.roll(base, 2 * WIDTH, 1)).astype(BF16)
+        for h in range(half // 512):
             at = slice(512 * h, 512 * h + 512)
             form(b_ref[0, :, :, at].reshape(512, 512), b_ref[1, :, :, at].reshape(512, 512),
-                 cb_ref[:, at], coef, stack_b, rb.at[:, at], sb.at[:, at])
-
-    tile = ra.shape[1]
-    form(a_ref[:, 0].reshape(512, tile), a_ref[:, 1].reshape(512, tile),
-         ca_ref[...], coef, stack_a, ra, sa)
+                 cb_ref[:, at], left[...], stack_b, rb.at[:, at], sb.at[:, at])
+        for h in range(tile // piece):
+            form_a(a0_ref, c0_ref, ra0, sa0, h)
+
     contract = (((0,), (0,)), ((), ()))
-    numer = lax.dot_general(ra[...], rb[...], contract, preferred_element_type=F32)
-    denom = lax.dot_general(sa[...], sb[...], contract, preferred_element_type=F32)
-    out_ref[...] = numer / denom
+
+    def phase(ra, sa, row, a_ref, c_ref, rn, sn):
+        for h in range(half // 256):
+            at = slice(256 * h, 256 * h + 256)
+            numer = lax.dot_general(ra[...], rb[:, at], contract, preferred_element_type=F32)
+            denom = lax.dot_general(sa[...], sb[:, at], contract, preferred_element_type=F32)
+            out_ref[row:row + tile, at] = numer / denom
+            if h < tile // piece:
+                form_a(a_ref, c_ref, rn, sn, h)
+
+    phase(ra0, sa0, 0, a1_ref, c1_ref, ra1, sa1)
+    phase(ra1, sa1, tile, a2_ref, c2_ref, ra0, sa0)
 
 
 def ratio(a_raw, b_raw, comps, comps_b, coef):
     people = comps.shape[1]
     half = people // 2
     tile = 256
+    tiles = people // tile
     whole = lambda shape: pl.BlockSpec(shape, lambda i: (0,) * len(shape), pipeline_mode=pl.Buffered(1))
+    first = lambda i: 0
+    odd = lambda i: 2 * i + 1
+    even = lambda i: jnp.minimum(2 * i + 2, tiles - 2)
+    a_spec = lambda at: pl.BlockSpec((16, 2, 32, tile), lambda i: (0, 0, 0, at(i)))
+    c_spec = lambda at: pl.BlockSpec((COMPS, tile), lambda i: (0, at(i)))
     return pl.pallas_call(
-        ratio_kernel,
+        functools.partial(ratio_kernel, tiles // 2),
         out_shape=jax.ShapeDtypeStruct((people, half), F32),
-        grid=(people // tile,),
+        grid=(tiles // 2,),
         in_specs=[
-            pl.BlockSpec((16, 2, 32, tile), lambda i: (0, 0, 0, i)),
+            pl.BlockSpec((16, 2, 32, tile), lambda i: (0, 0, 0, 0), pipeline_mode=pl.Buffered(1)),
+            a_spec(odd), a_spec(even),
             whole((2, 16, 32, half)),
-            pl.BlockSpec((COMPS, tile), lambda i: (0, i)),
+            pl.BlockSpec((COMPS, tile), lambda i: (0, 0), pipeline_mode=pl.Buffered(1)),
+            c_spec(odd), c_spec(even),
             whole((COMPS, half)),
             whole((512, 128)),
         ],
-        out_specs=pl.BlockSpec((tile, half), lambda i: (i, 0)),
+        out_specs=pl.BlockSpec((2 * tile, half), lambda i: (i, 0)),
         scratch_shapes=[
+            pltpu.VMEM((512, 256), BF16),
             pltpu.VMEM((512, half), BF16),
             pltpu.VMEM((512, half), BF16),
             pltpu.VMEM((512, tile), BF16),
             pltpu.VMEM((512, tile), BF16),
-            pltpu.VMEM((384, tile), F32),
-            pltpu.VMEM((384, 512), F32),
+            pltpu.VMEM((512, tile), BF16),
+            pltpu.VMEM((512, tile), BF16),
+            pltpu.VMEM((tile // 256, 256, 256), F32),
+            pltpu.VMEM((256, 512), F32),
         ],
         name="form_ratio",
-    )(a_raw, b_raw, comps, comps_b, coef)
+    )(a_raw, a_raw, a_raw, b_raw, comps, comps, comps, comps_b, coef)
 
 
 def per_device(dosage, present, comps):

time: 80.7 us -> 76 us (0.942)
  Pallas kernels: 80.4 us -> 75.9 us
    pallas_call x1, Pallas kernels: 23.2 us -> 18.7 us  [ratio(): pl.pallas_call(functools.partial(ratio_kernel, tiles // 2), out_shape=jax...]
where the time goes in v3:
time: 76 us; the launch traced here: 75.9 us
  Pallas kernels  75.9 us (100%)
    pallas_call x1, Pallas kernels, gather(): pl.pallas_call(gather_kernel, out_shape=(jax.ShapeDtypeStruct((16, 2, mar...  57.2 us
    pallas_call x1, Pallas kernels, ratio(): pl.pallas_call(functools.partial(ratio_kernel, tiles // 2), out_shape=jax...  18.7 us

profile of v3, /device:TPU:1, one launch (start us, length us, event | category | flops | bytes accessed | tf_op | source)
XLA Modules:
  0.0 75.9 jit_solution(18123250160014472761)
XLA Ops:
  0.0 57.2 %gather_fit.1 = (bf16[16,2,32,3072]{3,2,1,0:T(8,128)(2,1)}, bf16[2,16,32,1536]{3,2,1,0:T(8,128)(2,1)}, f32[32,1536]{1,0:T(8,128)}, f32[16,4,8,128]{3,2,1,0:T(8,128)}) custom-call(s32[32,3072]{1,0:T(8,128)} %dosage.1, s32[32,3072]{1,0:T(8,128)} %present.1, f32[32,3072]{1,0:T(8,128)} %c2_ref.1), custom_call_target="tpu_custom_call" | custom-call | tf_op jit(solution)/shard_map/gather_fit/pallas_call | solution.py:404
  57.2 18.7 %form_ratio.1 = f32[3072,1536]{1,0:T(8,128)} custom-call(bf16[16,2,32,3072]{3,2,1,0:T(8,128)(2,1)} %get-tuple-element.9.a0_ref.a1_ref.a2_ref, bf16[16,2,32,3072]{3,2,1,0:T(8,128)(2,1)} %get-tuple-element.9.a0_ref.a1_ref.a2_ref, bf16[16,2,32,3072]{3,2,1,0:T(8,128)(2,1)} %get-tuple-element.9.a0_ref.a1_ref.a2_ref, ...), custom_call_target="tpu_custom_call" | custom-call | tf_op jit(solution)/shard_map/form_ratio/pallas_call | solution.py:508

commit v4 on v3

--- a/solution.py
+++ b/solution.py
@@ -301,7 +301,7 @@
         right, left = b_one(p, zh_, yl, core_of[e]), b_one(p, zh_, yr, core_of[e])
         arrive(right, f"{tag}_yr{p}{e}")
         arrive(left, f"{tag}_yl{p}{e}")
-        if p == 0:
+        if e == 0:
             pass_on(right, f"{tag}_far{p}{e}", yr_dev)
         else:
             pass_on(left, f"{tag}_far{p}{e}", yl_dev)
@@ -309,12 +309,6 @@
     parts = [(p, e) for p in range(2) for e in range(2)]
     for p, e in parts:
         start_column(p, e)
-    for p, e in parts:
-        relay_column(p, e)
-    arrive_or_keep(home(0), piece(cb_out, y), "leg2_c_same")
-    pass_on(piece(cb_out, y), "c_yr", yr_dev)
-    pass_on(piece(cb_out, y), "c_yl", yl_dev)
-
     total = send[r % 4]
     for d in range(1, 8):
         arrive(recv.at[d], ("rs", d))
@@ -332,6 +326,12 @@
     keep_coef.start()
     for d in range(1, 4):
         push(coef, coef_out.at[c, y], ("cag", d), (row(zh, (y + d) % 4), c))
+
+    for p, e in parts:
+        relay_column(p, e)
+    arrive_or_keep(home(0), piece(cb_out, y), "leg2_c_same")
+    pass_on(piece(cb_out, y), "c_yr", yr_dev)
+    pass_on(piece(cb_out, y), "c_yl", yl_dev)
 
     for p in range(2):
         arrive(a_slot(zl, xl, k, p), f"own_xr{p}")

time: 76 us -> 75.6 us (level)
  Pallas kernels: 75.9 us -> 74.9 us
    pallas_call x1, Pallas kernels: 57.2 us -> 56.2 us  [gather(): pl.pallas_call(gather_kernel, out_shape=(jax.ShapeDtypeStruct((16, 2, mar...]
where the time goes in v4:
time: 75.6 us; the launch traced here: 74.9 us
  Pallas kernels  74.9 us (99%)
    pallas_call x1, Pallas kernels, gather(): pl.pallas_call(gather_kernel, out_shape=(jax.ShapeDtypeStruct((16, 2, mar...  56.2 us
    pallas_call x1, Pallas kernels, ratio(): pl.pallas_call(functools.partial(ratio_kernel, tiles // 2), out_shape=jax...  18.6 us

profile of v4, /device:TPU:1, one launch (start us, length us, event | category | flops | bytes accessed | tf_op | source)
XLA Modules:
  0.0 74.9 jit_solution(11352812092892873450)
XLA Ops:
  0.0 56.2 %gather_fit.1 = (bf16[16,2,32,3072]{3,2,1,0:T(8,128)(2,1)}, bf16[2,16,32,1536]{3,2,1,0:T(8,128)(2,1)}, f32[32,1536]{1,0:T(8,128)}, f32[16,4,8,128]{3,2,1,0:T(8,128)}) custom-call(s32[32,3072]{1,0:T(8,128)} %dosage.1, s32[32,3072]{1,0:T(8,128)} %present.1, f32[32,3072]{1,0:T(8,128)} %c2_ref.1), custom_call_target="tpu_custom_call" | custom-call | tf_op jit(solution)/shard_map/gather_fit/pallas_call | solution.py:404
  56.3 18.6 %form_ratio.1 = f32[3072,1536]{1,0:T(8,128)} custom-call(bf16[16,2,32,3072]{3,2,1,0:T(8,128)(2,1)} %get-tuple-element.9.a0_ref.a1_ref.a2_ref, bf16[16,2,32,3072]{3,2,1,0:T(8,128)(2,1)} %get-tuple-element.9.a0_ref.a1_ref.a2_ref, bf16[16,2,32,3072]{3,2,1,0:T(8,128)(2,1)} %get-tuple-element.9.a0_ref.a1_ref.a2_ref, ...), custom_call_target="tpu_custom_call" | custom-call | tf_op jit(solution)/shard_map/form_ratio/pallas_call | solution.py:508
